TPU v7x, 32 devices: a whole 2x2x4 slice. The times are simulated.
32 devices in a mesh: layer: 2 (over y), row: 4 (over z), col: 4 (over x, core).
Axes of the slice: x: 2, y: 2, z: 4, core: 2. Of those that a mesh axis runs over, the one named last changes fastest.
Arguments:
- leaf_sol: bfloat16 [8, 256, 256], P(('layer', 'col'), 'row'), may hold values from -6 to 6
- lower_blocks: bfloat16 [8192, 1024], P(('layer', 'row'), 'col'), may hold values from -0.1875 to 0.1875
- lower_mask: int32 [32, 4], P(('layer', 'row'), 'col'), may hold values 0 or 1
- upper_blocks: bfloat16 [2048, 4096], P(('layer', 'col'), 'row'), may hold values from -0.125 to 0.125
- upper_mask: int32 [8, 16], P(('layer', 'col'), 'row'), may hold values 0 or 1
- anc_rhs: bfloat16 [4096, 256], P(('row', 'col')), may hold values from -6 to 6
- diag_inv: bfloat16 [4096, 256], P(('row', 'col')), may hold values from -0.375 to 0.375
Outputs:
- new_leaves: bfloat16 [8, 256, 256], P(('layer', 'col'), 'row')
- anc_sol: bfloat16 [4096, 256], P(('row', 'col'))
Inputs may be any that keep to these rules, and one draw needn't show every extreme that they name: `lower_mask`: 1 marks a stored block of L. `upper_mask`: 1 marks a stored block of U.
All inputs are finite; a program needn't handle non-finite values.
Results may differ from a plain program's by a relative error of at most 0.0044.
Values may be sent and summed in bfloat16 or wider, within the bound.
A program may use at most 64 MiB of HBM per device.

v0:
```python
import jax
import jax.numpy as jnp
from jax import lax
from jax.sharding import PartitionSpec as P


def expand(mask, block):
    first, second = mask.shape
    full = jnp.broadcast_to(mask[:, None, :, None], (first, block, second, block))
    return full.reshape(first * block, second * block)


def shards(leaf_sol, lower_blocks, lower_mask, upper_blocks, upper_mask, anc_rhs, diag_inv):
    block = diag_inv.shape[1]
    width = leaf_sol.shape[2]
    lower_masked = lower_blocks * expand(lower_mask, block).astype(jnp.bfloat16)
    upper_masked = upper_blocks * expand(upper_mask, block).astype(jnp.bfloat16)
    columns = lower_masked
    term = lax.dot_general(
        lax.all_gather(leaf_sol, "row", axis=1, tiled=True)[0],
        columns,
        (((0,), (1,)), ((), ())),
        preferred_element_type=jnp.float32,
    )
    inverse = diag_inv.astype(jnp.float32)
    layers = lax.axis_size("layer")
    columns = lax.axis_size("col")
    slice_width = width // layers
    pieces = term.reshape(layers, slice_width, columns, block)
    pieces = pieces.transpose(0, 2, 1, 3).reshape(layers * columns, slice_width, block)
    summed = lax.psum_scatter(pieces, ("layer", "col"), scatter_dimension=0, tiled=True)[0]
    layer_index = lax.axis_index("layer")
    rhs_part = lax.dynamic_slice_in_dim(anc_rhs, layer_index * slice_width, slice_width, 1)
    remain = rhs_part.astype(jnp.float32).T - summed
    solved_part = lax.dot_general(
        remain,
        inverse,
        (((1,), (1,)), ((), ())),
        precision=lax.Precision.HIGHEST,
        preferred_element_type=jnp.float32,
    ).astype(jnp.bfloat16)
    gathered_sides = lax.all_gather(solved_part, "layer", axis=0, tiled=True)
    anc_sol = gathered_sides.T
    columns = upper_masked
    folded = jnp.dot(
        columns,
        lax.all_gather(anc_sol, "col", axis=0, tiled=True),
        preferred_element_type=jnp.float32,
    )
    correct = lax.psum_scatter(folded, "row", scatter_dimension=0, tiled=True)
    new_leaves = (leaf_sol[0].astype(jnp.float32) - correct).astype(jnp.bfloat16)
    return (new_leaves.reshape(leaf_sol.shape), anc_sol)


def solution(mesh):
    in_specs = (
        P(("layer", "col"), "row", None),
        P(("layer", "row"), "col"),
        P(("layer", "row"), "col"),
        P(("layer", "col"), "row"),
        P(("layer", "col"), "row"),
        P(("row", "col"), None),
        P(("row", "col"), None),
    )
    out_specs = (P(("layer", "col"), "row", None), P(("row", "col"), None))
    return jax.shard_map(shards, mesh=mesh, in_specs=in_specs, out_specs=out_specs, check_vma=False)
```

profile of v0, /device:TPU:0, one launch (start us, length us, event | category | flops | bytes accessed | tf_op | source)
XLA Modules:
  0.0 106.7 jit_solution(17108516704674506642)
XLA Ops:
  7.2 0.0 copy-start
  7.2 0.0 reduce-scatter.3.cloned.1.call-start
  7.2 0.7 convert_bitcast_fusion
  7.9 0.1 broadcast_bitcast_fusion
  8.0 15.3 %all_gather.9 = bf16[1,256,256]{2,1,0:T(8,128)(2,1)S(1)} all-gather(bf16[1,64,256]{2,1,0:T(8,128)(2,1)} %param.7), channel_id=1, replica_groups=mesh['layer'=2,'row'=4,'col'=4] {'row'}, dimensions={1}, use_global_device_ids=true | all-gather | bytes 163840 | tf_op jit(solution)/shard_map/all_gather | solution.py:20
  23.3 1.4 %convolution_bitcast_fusion = f32[256,1024]{0,1:T(8,128)S(1)} fusion(bf16[1024,256]{1,0:T(8,128)(2,1)} %param.8, bf16[1024]{0:T(1024)(128)(2,1)S(1)} %bitcast.40, bf16[1,256,256]{2,1,0:T(8,128)(2,1)S(1)} %all_gather.9), kind=kOutput, calls=%fused_computation | convolution fusion | flops 134479872 | bytes 1705984 | tf_op jit(solution)/shard_map/dot_general | solution.py:19
  24.7 0.5 reshape.29
  25.2 1.0 copy.9
  26.3 0.0 reduce-scatter.3.cloned.1.call-update
  26.3 0.0 reduce-scatter.5.cloned.1.call-start
  26.4 0.0 copy-start.4
  26.4 0.6 copy-done.4
  27.0 0.1 broadcast_bitcast_fusion.1
  27.1 36.6 %reduce-scatter.3.cloned.1.call-done = f32[1,128,256]{1,2,0:T(8,128)} async-done(((f32[8,128,256]{1,2,0:T(8,128)}), f32[1,128,256]{1,2,0:T(8,128)}) %reduce-scatter.3.cloned.1.call-update) | async-done | bytes 131088 | tf_op jit(solution)/shard_map/reduce_scatter | solution.py:31
  63.7 1.2 %convolution_convert_fusion = bf16[128,256]{1,0:T(8,128)(2,1)S(1)} fusion(bf16[256,256]{1,0:T(8,128)(2,1)S(1)} %copy-done, f32[1,128,256]{1,2,0:T(8,128)} %reduce-scatter.3.cloned.1.call-done, bf16[256,256]{1,0:T(8,128)(2,1)S(1)} %copy-done.3, s32[]{:T(128)S(6)} %select_n.3), kind=kOutput, calls=%fused_computation.1 | convolution fusion | flops 100761600 | bytes 393220 | tf_op jit(solution)/shard_map/dot_general | solution.py:35
  65.0 0.0 copy-start.1
  65.0 5.1 %all_gather.10 = bf16[256,256]{1,0:T(8,128)(2,1)S(1)} all-gather(bf16[128,256]{1,0:T(8,128)(2,1)S(1)} %convolution_convert_fusion), channel_id=1, replica_groups=mesh['layer'=2,'row'=4,'col'=4] {'layer'}, dimensions={0}, use_global_device_ids=true | all-gather | bytes 196608 | tf_op jit(solution)/shard_map/all_gather | solution.py:42
  70.0 7.1 %all_gather.11 = bf16[1024,256]{0,1:T(8,128)(2,1)S(1)} all-gather(bf16[256,256]{0,1:T(8,128)(2,1)S(1)} %bitcast.37), channel_id=1, replica_groups=mesh['layer'=2,'row'=4,'col'=4] {'col'}, dimensions={0}, use_global_device_ids=true | all-gather | bytes 655360 | tf_op jit(solution)/shard_map/all_gather | solution.py:47
  77.2 1.0 fusion.1
  78.2 0.0 reduce-scatter.5.cloned.1.call-update
  78.2 0.0 copy-start.2
  78.2 0.8 copy.10
  79.0 19.4 %reduce-scatter.5.cloned.1.call-done = f32[64,256]{1,0:T(8,128)} async-done(((f32[256,256]{1,0:T(8,128)}), f32[64,256]{1,0:T(8,128)}) %reduce-scatter.5.cloned.1.call-update) | async-done | bytes 65552 | tf_op jit(solution)/shard_map/reduce_scatter | solution.py:50
  98.4 1.5 %fusion.10 = bf16[1,64,256]{2,1,0:T(8,128)(2,1)} fusion(f32[64,256]{1,0:T(8,128)} %reduce-scatter.5.cloned.1.call-done, bf16[1,64,256]{2,1,0:T(8,128)(2,1)S(1)} %copy-done.2), kind=kLoop, calls=%fused_computation.14 | loop fusion | flops 49152 | bytes 131072 | tf_op jit(solution)/shard_map/reshape | solution.py:52
  (8 shorter events, 0.0 us)
Async XLA Ops:
  7.2 56.6 %copy-start = (bf16[256,256]{1,0:T(8,128)(2,1)S(1)}, bf16[256,256]{1,0:T(8,128)(2,1)}, u32[]{:S(2)}) copy-start(bf16[256,256]{1,0:T(8,128)(2,1)} %param.13) | copy-start | bytes 393220
  7.2 56.6 %reduce-scatter.3.cloned.1.call-start = ((), (), s32[]{:S(2)}) async-start(), calls=%async_computation.2 | async-start | bytes 1179648 | tf_op jit(solution)/shard_map/reduce_scatter | solution.py:31
  26.3 37.5 %copy-start.3 = (bf16[256,256]{1,0:T(8,128)(2,1)S(1)}, bf16[256,256]{1,0:T(8,128)(2,1)}, u32[]{:S(2)}) copy-start(bf16[256,256]{1,0:T(8,128)(2,1)} %param.12) | copy-start | bytes 393220
  26.3 72.1 %reduce-scatter.5.cloned.1.call-start = ((), (), s32[]{:S(2)}) async-start(), calls=%async_computation.3 | async-start | bytes 327680 | tf_op jit(solution)/shard_map/reduce_scatter | solution.py:50
  26.4 0.7 copy-start.4
  65.0 12.2 %copy-start.1 = (bf16[256,1024]{1,0:T(8,128)(2,1)S(1)}, bf16[256,1024]{1,0:T(8,128)(2,1)}, u32[]{:S(2)}) copy-start(bf16[256,1024]{1,0:T(8,128)(2,1)} %param.10) | copy-start | bytes 1572868
  78.2 20.1 %copy-start.2 = (bf16[1,64,256]{2,1,0:T(8,128)(2,1)S(1)}, bf16[1,64,256]{2,1,0:T(8,128)(2,1)}, u32[]{:S(2)}) copy-start(bf16[1,64,256]{2,1,0:T(8,128)(2,1)} %param.7) | copy-start | bytes 98308
Sparse Core Ops, SparseCore 0:
  26.4 37.2 reduce-scatter.2
  78.3 19.9 reduce-scatter.4
where the time goes:
time: 107 us
  waiting for transfers between devices  56 us (52%)
  blocking collectives  27.5 us (26%)
  between operations  14.1 us (13%)
  matrix products  3.63 us (3%)
  local copies, waits for them, and re-layouts  3.19 us (3%)
  other arithmetic  2.15 us (2%)
    reduce_scatter x1, waiting for transfers between devices, shards(): lax.psum_scatter(pieces, ('layer', 'col'), scatter_dimension=0, tiled=True)  36.6 us
    reduce_scatter x1, waiting for transfers between devices, shards(): correct = lax.psum_scatter(folded, 'row', scatter_dimension=0, tiled=True)  19.4 us
    all_gather x1, blocking collectives, shards(): lax.all_gather(leaf_sol, 'row', axis=1, tiled=True)[0]  15.3 us
    all_gather x1, blocking collectives, shards(): lax.all_gather(anc_sol, 'col', axis=0, tiled=True)  7.13 us
    all_gather x1, blocking collectives, shards(): gathered_sides = lax.all_gather(solved_part, 'layer', axis=0, tiled=True)  5.07 us
  transfers between devices with their start and end apart: 2, of which 2 were waited for; matrix products, arithmetic and copies ran while one was open for 1% of the time, Pallas kernels for 0%

commit v1 on v0

--- a/solution.py
+++ b/solution.py
@@ -17,7 +17,7 @@
     upper_masked = upper_blocks * expand(upper_mask, block).astype(jnp.bfloat16)
     columns = lower_masked
     term = lax.dot_general(
-        lax.all_gather(leaf_sol, "row", axis=1, tiled=True)[0],
+        jnp.concatenate(lax.all_gather(leaf_sol, "row"), axis=1)[0],
         columns,
         (((0,), (1,)), ((), ())),
         preferred_element_type=jnp.float32,

time: 107 us -> 106 us (level)
  no operation moved by 1% of the time
where the time goes in v1:
time: 106 us
  waiting for transfers between devices  56.1 us (53%)
  blocking collectives  27.5 us (26%)
  between operations  14.1 us (13%)
  matrix products  3.64 us (3%)
  local copies, waits for them, and re-layouts  3.19 us (3%)
  other arithmetic  1.47 us (1%)
    reduce_scatter x1, waiting for transfers between devices, shards(): lax.psum_scatter(pieces, ('layer', 'col'), scatter_dimension=0, tiled=True)  36.7 us
    reduce_scatter x1, waiting for transfers between devices, shards(): correct = lax.psum_scatter(folded, 'row', scatter_dimension=0, tiled=True)  19.4 us
    all_gather x1, blocking collectives, shards(): lax.all_gather(leaf_sol, 'row')  15.3 us
    all_gather x1, blocking collectives, shards(): lax.all_gather(anc_sol, 'col', axis=0, tiled=True)  7.13 us
    all_gather x1, blocking collectives, shards(): gathered_sides = lax.all_gather(solved_part, 'layer', axis=0, tiled=True)  5.07 us
  transfers between devices with their start and end apart: 2, of which 2 were waited for; matrix products, arithmetic and copies ran while one was open for 1% of the time, Pallas kernels for 0%

profile of v1, /device:TPU:0, one launch (start us, length us, event | category | flops | bytes accessed | tf_op | source)
XLA Modules:
  0.0 106.0 jit_solution(8842433339759830636)
XLA Ops:
  7.2 0.0 copy-start
  7.2 0.0 reduce-scatter.3.cloned.1.call-start
  7.2 15.3 %all-gather = bf16[4,64,256]{2,1,0:T(8,128)(2,1)S(1)} all-gather(bf16[1,64,256]{2,1,0:T(8,128)(2,1)} %param.7), channel_id=2, replica_groups=mesh['layer'=2,'row'=4,'col'=4] {'row'}, dimensions={0}, use_global_device_ids=true | all-gather | bytes 163840 | tf_op jit(solution)/shard_map/all_gather | solution.py:20
  22.5 0.1 broadcast_bitcast_fusion
  22.6 1.4 %convolution_bitcast_fusion = f32[256,1024]{0,1:T(8,128)S(1)} fusion(bf16[256,256]{1,0:T(8,128)(2,1)S(1)} %bitcast.38, bf16[1024,256]{1,0:T(8,128)(2,1)} %param.8, bf16[1024]{0:T(1024)(128)(2,1)S(1)} %bitcast.40), kind=kOutput, calls=%fused_computation | convolution fusion | flops 134479872 | bytes 1705984 | tf_op jit(solution)/shard_map/dot_general | solution.py:19
  24.0 0.5 reshape.29
  24.6 1.0 copy.11
  25.6 0.0 reduce-scatter.3.cloned.1.call-update
  25.6 0.0 reduce-scatter.5.cloned.1.call-start
  25.7 0.0 copy-start.5
  25.7 0.6 copy-done.5
  26.4 0.1 broadcast_bitcast_fusion.1
  26.4 36.7 %reduce-scatter.3.cloned.1.call-done = f32[1,128,256]{1,2,0:T(8,128)} async-done(((f32[8,128,256]{1,2,0:T(8,128)}), f32[1,128,256]{1,2,0:T(8,128)}) %reduce-scatter.3.cloned.1.call-update) | async-done | bytes 131088 | tf_op jit(solution)/shard_map/reduce_scatter | solution.py:31
  63.1 0.0 copy-done.3
  63.1 1.2 %convolution_convert_fusion = bf16[128,256]{1,0:T(8,128)(2,1)S(1)} fusion(bf16[256,256]{1,0:T(8,128)(2,1)S(1)} %copy-done, f32[1,128,256]{1,2,0:T(8,128)} %reduce-scatter.3.cloned.1.call-done, bf16[256,256]{1,0:T(8,128)(2,1)S(1)} %copy-done.3, s32[]{:T(128)S(6)} %select_n.3), kind=kOutput, calls=%fused_computation.1 | convolution fusion | flops 100761600 | bytes 393220 | tf_op jit(solution)/shard_map/dot_general | solution.py:35
  64.3 0.0 copy-start.1
  64.3 5.1 %all_gather.14 = bf16[256,256]{1,0:T(8,128)(2,1)S(1)} all-gather(bf16[128,256]{1,0:T(8,128)(2,1)S(1)} %convolution_convert_fusion), channel_id=1, replica_groups=mesh['layer'=2,'row'=4,'col'=4] {'layer'}, dimensions={0}, use_global_device_ids=true | all-gather | bytes 196608 | tf_op jit(solution)/shard_map/all_gather | solution.py:42
  69.4 7.1 %all_gather.15 = bf16[1024,256]{0,1:T(8,128)(2,1)S(1)} all-gather(bf16[256,256]{0,1:T(8,128)(2,1)S(1)} %bitcast.36), channel_id=1, replica_groups=mesh['layer'=2,'row'=4,'col'=4] {'col'}, dimensions={0}, use_global_device_ids=true | all-gather | bytes 655360 | tf_op jit(solution)/shard_map/all_gather | solution.py:47
  76.5 1.0 fusion.1
  77.6 0.0 reduce-scatter.5.cloned.1.call-update
  77.6 0.0 copy-start.2
  77.6 0.8 copy.12
  78.4 19.4 %reduce-scatter.5.cloned.1.call-done = f32[64,256]{1,0:T(8,128)} async-done(((f32[256,256]{1,0:T(8,128)}), f32[64,256]{1,0:T(8,128)}) %reduce-scatter.5.cloned.1.call-update) | async-done | bytes 65552 | tf_op jit(solution)/shard_map/reduce_scatter | solution.py:50
  97.7 1.5 %fusion.9 = bf16[1,64,256]{2,1,0:T(8,128)(2,1)} fusion(f32[64,256]{1,0:T(8,128)} %reduce-scatter.5.cloned.1.call-done, bf16[1,64,256]{2,1,0:T(8,128)(2,1)S(1)} %copy-done.2), kind=kLoop, calls=%fused_computation.13 | loop fusion | flops 49152 | bytes 131072 | tf_op jit(solution)/shard_map/reshape | solution.py:52
  (10 shorter events, 0.0 us)
Async XLA Ops:
  7.2 55.9 %copy-start = (bf16[256,256]{1,0:T(8,128)(2,1)S(1)}, bf16[256,256]{1,0:T(8,128)(2,1)}, u32[]{:S(2)}) copy-start(bf16[256,256]{1,0:T(8,128)(2,1)} %param.13) | copy-start | bytes 393220
  7.2 15.4 %copy-start.4 = (s32[4,1]{0,1:T(1,128)S(1)}, s32[4,1]{0,1:T(1,128)}, u32[]{:S(2)}) copy-start(s32[4,1]{0,1:T(1,128)} %param.9) | copy-start | bytes 52
  7.2 55.9 %reduce-scatter.3.cloned.1.call-start = ((), (), s32[]{:S(2)}) async-start(), calls=%async_computation.2 | async-start | bytes 1179648 | tf_op jit(solution)/shard_map/reduce_scatter | solution.py:31
  25.6 37.5 %copy-start.3 = (bf16[256,256]{1,0:T(8,128)(2,1)S(1)}, bf16[256,256]{1,0:T(8,128)(2,1)}, u32[]{:S(2)}) copy-start(bf16[256,256]{1,0:T(8,128)(2,1)} %param.12) | copy-start | bytes 393220
  25.6 72.1 %reduce-scatter.5.cloned.1.call-start = ((), (), s32[]{:S(2)}) async-start(), calls=%async_computation.3 | async-start | bytes 327680 | tf_op jit(solution)/shard_map/reduce_scatter | solution.py:50
  25.7 0.7 copy-start.5
  64.3 12.2 %copy-start.1 = (bf16[256,1024]{1,0:T(8,128)(2,1)S(1)}, bf16[256,1024]{1,0:T(8,128)(2,1)}, u32[]{:S(2)}) copy-start(bf16[256,1024]{1,0:T(8,128)(2,1)} %param.10) | copy-start | bytes 1572868
  77.6 20.1 %copy-start.2 = (bf16[1,64,256]{2,1,0:T(8,128)(2,1)S(1)}, bf16[1,64,256]{2,1,0:T(8,128)(2,1)}, u32[]{:S(2)}) copy-start(bf16[1,64,256]{2,1,0:T(8,128)(2,1)} %param.7) | copy-start | bytes 98308
Sparse Core Ops, SparseCore 0:
  25.8 37.2 reduce-scatter.2
  77.7 19.9 reduce-scatter.4
